TPU v7x, 512 devices: a whole 4x4x16 slice. The times are simulated.
512 devices in a mesh: replica: 64 (over x_lo, z, core), tensor: 8 (over x_hi, y).
Axes of the slice: x: 4 (x_hi: 2, x_lo: 2; x = x_hi * 2 + x_lo), y: 4, z: 16, core: 2. Of those that a mesh axis runs over, the one named last changes fastest.
Arguments:
- qkv_weight: bfloat16 [5120, 7168], P(('replica', 'tensor')), may hold values from -0.078125 to 0.078125
- qkv_bias: bfloat16 [7168], P('tensor'), may hold values from -7 to 7
- norm_gain: bfloat16 [5120], replicated, may hold values from 0.099609375 to 1.8984375
- decode_hidden: bfloat16 [1024, 5120], P('replica'), may hold values from -6 to 6
- stored_keys: bfloat16 [1024, 8, 256, 128], P('replica', 'tensor'), may hold values from -72 to 72
- stored_values: bfloat16 [1024, 8, 256, 128], P('replica', 'tensor'), may hold values from -6 to 6
- stored_lengths: int32 [64, 16], P('replica'), may hold values from 1 to 256, 2048 in all within a row
- response_hidden: bfloat16 [640, 64, 5120], P('replica', None, 'tensor'), may hold values from -6 to 6
- response_lengths: int32 [64, 10], P('replica'), may hold values from 1 to 64, 560 in all within a row
- response_target: int32 [640, 1], P('replica'), may hold values from 0 to 7; in each aligned block of 10 rows (0 to 9, 10 to 19, ...) at most 2 rows name the same one
Outputs:
- step_attention: bfloat16 [1024, 5120], P('replica', 'tensor')
- learner_attention: bfloat16 [1024, 64, 5120], P(('replica', 'tensor'))
Inputs may be any that keep to these rules, and one draw needn't show every extreme that they name: `response_lengths`: the 10 lengths of one group sum to 560, and one of them equals 64. `stored_lengths`: the 16 lengths of one group sum to 2048, and one of them equals 256. `response_target`: among the 10 responses of one rollout group at most 2 name the same learner device, and in some groups one device is named by exactly 2.
All inputs are finite; a program needn't handle non-finite values.
Results may differ from a plain program's by a relative error of at most 0.0065.
The roundings to bfloat16 on the way count: a program that leaves them out, or rounds other values in their place, can miss the bound.
Values may be sent and summed in bfloat16 or wider, within the bound.
A program may use at most 64 MiB of HBM per device.

v0:
```python
import math
import jax
import jax.numpy as jnp
from jax import lax
from jax.sharding import PartitionSpec as P

MODEL_WIDTH = 5120
QUERY_HEADS = 40
KV_HEADS = 8
HEAD_DIM = 128
DONE_PER_GROUP = 10
RESPONSE_LIMIT = 64


def normalize(rows_in, gain_vec):
    widened = rows_in.astype(jnp.float32)
    inverse = lax.rsqrt(jnp.mean(widened * widened, axis=-1, keepdims=True) + 1e-06)
    return (widened * inverse * gain_vec.astype(jnp.float32)).astype(jnp.bfloat16)


def block_attend(qkv_rows, token_lengths):
    rollout_groups = qkv_rows.shape[3] - 2
    head_size = qkv_rows.shape[4]
    number = qkv_rows.shape[0]
    length = qkv_rows.shape[1]
    query = qkv_rows[:, :, :, :rollout_groups]
    key_matrix = qkv_rows[:, :, :, rollout_groups]
    value_matrix = qkv_rows[:, :, :, rollout_groups + 1]
    scores = jnp.einsum(
        "nikgh,njkh->nkgij", query, key_matrix, preferred_element_type=jnp.float32
    ) / math.sqrt(head_size)
    causal = jnp.arange(length)[None, :] <= jnp.arange(length)[:, None]
    masked = jnp.where(causal, scores, -jnp.inf)
    peak = jnp.max(masked, axis=-1, keepdims=True)
    powers = jnp.where(causal, jnp.exp(scores - peak), 0.0)
    probs = (powers / jnp.sum(powers, axis=-1, keepdims=True)).astype(jnp.bfloat16)
    mixture = jnp.einsum(
        "nkgij,njkh->nikgh", probs, value_matrix, preferred_element_type=jnp.float32
    )
    in_range = jnp.arange(length)[None, :] < token_lengths[:, None]
    mixture = jnp.where(in_range[:, :, None, None, None], mixture, 0.0)
    return mixture.astype(jnp.bfloat16).reshape(number, length, -1)


def attend_decoding(qkv_rows, key_cache, value_cache, token_lengths):
    rollout_groups = qkv_rows.shape[2] - 2
    head_size = qkv_rows.shape[3]
    number = qkv_rows.shape[0]
    query = qkv_rows[:, :, :rollout_groups]
    new_key = qkv_rows[:, :, rollout_groups]
    new_value = qkv_rows[:, :, rollout_groups + 1]
    scores = jnp.einsum(
        "bkgh,bklh->bkgl", query, key_cache, preferred_element_type=jnp.float32
    ) / math.sqrt(head_size)
    self_score = jnp.einsum("bkgh,bkh->bkg", query, new_key, preferred_element_type=jnp.float32)[
        ..., None
    ] / math.sqrt(head_size)
    filled = (jnp.arange(key_cache.shape[2])[None, :] < token_lengths[:, None])[:, None, None, :]
    peak = jnp.maximum(
        jnp.max(jnp.where(filled, scores, -jnp.inf), axis=-1, keepdims=True), self_score
    )
    powers = jnp.where(filled, jnp.exp(scores - peak), 0.0)
    self_power = jnp.exp(self_score - peak)
    total = jnp.sum(powers, axis=-1, keepdims=True) + self_power
    probs = (powers / total).astype(jnp.bfloat16)
    self_prob = (self_power / total).astype(jnp.bfloat16)
    mixture = jnp.einsum("bkgl,bklh->bkgh", probs, value_cache, preferred_element_type=jnp.float32)
    mixture = mixture + self_prob.astype(jnp.float32) * new_value.astype(jnp.float32)[:, :, None, :]
    return mixture.astype(jnp.bfloat16).reshape(number, -1)


def selector(targets, shards, slot_capacity):
    number = targets.shape[0]
    same_dest = targets[:, None] == targets[None, :]
    earlier = jnp.arange(number)[None, :] < jnp.arange(number)[:, None]
    slot_index = jnp.sum((same_dest & earlier).astype(jnp.int32), axis=1)
    target_slot = targets * slot_capacity + slot_index
    return (
        jnp.arange(shards * slot_capacity, dtype=jnp.int32)[:, None] == target_slot[None, :]
    ).astype(jnp.int32)


def body(
    qkv_weight,
    qkv_bias,
    norm_gain,
    decode_hidden,
    stored_keys,
    stored_values,
    stored_lengths,
    response_hidden,
    response_lengths,
    response_target,
):
    tensor_count = lax.axis_size("tensor")
    rollout_groups = QUERY_HEADS // KV_HEADS
    slot_capacity = DONE_PER_GROUP // tensor_count + 1
    rows_local = qkv_weight.shape[0]
    col_width = qkv_weight.shape[1] // tensor_count
    local_groups = col_width // ((rollout_groups + 2) * HEAD_DIM)
    blocks = lax.all_to_all(
        qkv_weight.reshape(rows_local, tensor_count, col_width),
        "tensor",
        split_axis=1,
        concat_axis=0,
        tiled=True,
    )
    blocks = blocks.reshape(rows_local * tensor_count, col_width)
    step_norm = normalize(decode_hidden, norm_gain)
    resp_full = lax.all_gather(response_hidden, "tensor", axis=2, tiled=True)
    resp_norm = normalize(resp_full, norm_gain).reshape(
        DONE_PER_GROUP * RESPONSE_LIMIT, MODEL_WIDTH
    )
    weight_all = lax.all_gather(blocks, "replica", axis=0, tiled=True)
    step_acc = jnp.dot(step_norm, weight_all, preferred_element_type=jnp.float32)
    resp_acc = jnp.dot(resp_norm, weight_all, preferred_element_type=jnp.float32)
    offset = qkv_bias.astype(jnp.float32)
    decode_projected = (
        (step_acc + offset)
        .astype(jnp.bfloat16)
        .reshape(-1, local_groups, rollout_groups + 2, HEAD_DIM)
    )
    response_projected = (
        (resp_acc + offset).astype(jnp.bfloat16).reshape(DONE_PER_GROUP, RESPONSE_LIMIT, col_width)
    )
    decode_output = attend_decoding(
        decode_projected, stored_keys, stored_values, stored_lengths.reshape(-1)
    )
    token_lengths = response_lengths.reshape(DONE_PER_GROUP)
    targets = response_target.reshape(DONE_PER_GROUP)
    chooser = selector(targets, tensor_count, slot_capacity)
    mine = lax.dynamic_slice_in_dim(
        chooser, lax.axis_index("tensor") * slot_capacity, slot_capacity, 0
    )
    slot_lens = jnp.sum(mine * token_lengths[None, :], axis=1)
    chooser_cube = chooser.astype(jnp.bfloat16).reshape(tensor_count, slot_capacity, DONE_PER_GROUP)
    sendbuf = jnp.einsum(
        "dcj,jrw->crdw", chooser_cube, response_projected, preferred_element_type=jnp.float32
    ).astype(jnp.bfloat16)
    received_rows = lax.all_to_all(sendbuf, "tensor", split_axis=2, concat_axis=2, tiled=True)
    received_rows = received_rows.reshape(
        slot_capacity, RESPONSE_LIMIT, KV_HEADS, rollout_groups + 2, HEAD_DIM
    )
    learner_out = block_attend(received_rows, slot_lens)
    return (decode_output, learner_out)


def solution(mesh):
    return jax.shard_map(
        body,
        mesh=mesh,
        in_specs=(
            P(("replica", "tensor"), None),
            P("tensor"),
            P(),
            P("replica", None),
            P("replica", "tensor", None, None),
            P("replica", "tensor", None, None),
            P("replica", None),
            P("replica", None, "tensor"),
            P("replica", None),
            P("replica", None),
        ),
        out_specs=(P("replica", "tensor"), P(("replica", "tensor"), None, None)),
        check_vma=False,
    )
```

profile of v0, /device:TPU:1, one launch (start us, length us, event | category | flops | bytes accessed | tf_op | source)
XLA Modules:
  0.0 312.3 jit_solution(8639920904462327456)
XLA Ops:
  7.2 0.0 copy-start
  7.2 0.0 copy-start.4
  7.2 0.0 copy-start.3
  7.2 0.0 copy-start.7
  7.2 0.0 copy-start.6
  7.2 0.0 copy-start.2
  7.2 0.0 copy-start.5
  7.2 0.0 all-gather.5.cloned.1.call-start
  7.3 0.7 all-gather.5.cloned.1.call-update
  8.0 0.0 all-gather.3.cloned.1.call-start
  8.0 1.0 copy.58
  9.0 14.8 %all_to_all.20 = bf16[10,8,896]{2,0,1:T(8,128)(2,1)S(1)} all-to-all(bf16[10,8,896]{2,0,1:T(8,128)(2,1)S(1)} %copy.38), channel_id=1, replica_groups=mesh['replica'=64,'tensor'=8] {'tensor'}, dimensions={1} | all-to-all | bytes 286720 | tf_op jit(solution)/shard_map/all_to_all | solution.py:101
  23.8 0.7 reshape.186
  24.5 0.0 all-gather.3.cloned.1.call-update
  24.5 0.0 copy-done.4
  24.6 0.0 copy-done.3
  24.6 0.0 copy-done.7
  24.6 0.2 convert_reduce_fusion
  24.8 0.0 copy-done.6
  24.8 0.1 fusion.42
  24.9 0.0 copy-done.2
  25.0 0.2 fusion.22
  25.1 0.1 iota_compare_fusion.3
  25.2 0.0 copy-done.5
  25.2 0.1 iota_compare_fusion.1
  25.3 96.4 %all-gather.5.cloned.1.call-done = bf16[10,64,5120]{2,1,0:T(8,128)(2,1)} async-done(((bf16[10,64,640]{2,1,0:T(8,128)(2,1)}), bf16[10,64,5120]{2,1,0:T(8,128)(2,1)}) %all-gather.5.cloned.1.call-update) | async-done | bytes 6553616 | tf_op jit(solution)/shard_map/all_gather | solution.py:110
  121.7 0.0 copy-start.1
  121.7 4.4 %fusion.1 = f32[10,64]{1,0:T(8,128)S(1)} fusion(bf16[10,64,5120]{2,1,0:T(8,128)(2,1)} %all-gather.5.cloned.1.call-done), kind=kLoop, calls=%fused_computation.3 | loop fusion | flops 9829760 | bytes 6556160 | tf_op jit(solution)/shard_map/reduce_sum | solution.py:17
  126.1 0.4 copy-done.1
  126.4 5.3 %fusion.3 = bf16[10,64,5120]{2,1,0:T(8,128)(2,1)} fusion(bf16[10,64,5120]{2,1,0:T(8,128)(2,1)S(1)} %copy-done.1, f32[5120]{0:T(1024)S(1)} %convert_element_type.82, f32[10,64]{1,0:T(8,128)S(1)} %add_rsqrt_fusion), kind=kLoop, calls=%fused_computation.5 | loop fusion | flops 13107200 | bytes 13130240 | tf_op jit(solution)/shard_map/convert_element_type | solution.py:18
  131.7 121.0 %all-gather.3.cloned.1.call-done = bf16[5120,896]{1,0:T(8,128)(2,1)} async-done(((bf16[80,896]{1,0:T(8,128)(2,1)}), bf16[5120,896]{1,0:T(8,128)(2,1)}) %all-gather.3.cloned.1.call-update) | async-done | bytes 9175056 | tf_op jit(solution)/shard_map/all_gather | solution.py:114
  252.8 11.8 %add_convert_fusion = bf16[640,896]{1,0:T(8,128)(2,1)S(1)} fusion(bf16[640,5120]{1,0:T(8,128)(2,1)} %bitcast.81, bf16[5120,896]{1,0:T(8,128)(2,1)} %all-gather.3.cloned.1.call-done, f32[896]{0:T(1024)S(1)} %convert_element_type.84), kind=kOutput, calls=%fused_computation.14 | convolution fusion | flops 5873172480 | bytes 16879104 | tf_op jit(solution)/shard_map/dot_general | solution.py:116
  264.5 0.9 convert_bitcast_fusion
  265.5 2.7 copy.40
  268.1 6.4 %all-to-all-start.1 = ((bf16[2,64,8,896]{3,0,1,2:T(2,128)(2,1)}), bf16[2,64,8,896]{3,0,1,2:T(2,128)(2,1)S(1)}, u32[]{:S(2)}, u32[]{:S(2)}) async-start(bf16[2,64,8,896]{3,0,1,2:T(2,128)(2,1)} %copy.40), calls=%async_computation.1 | async-start | bytes 3670016 | tf_op jit(solution)/shard_map/all_to_all | solution.py:140
  274.6 4.9 %fusion.19 = bf16[16,896]{1,0:T(8,128)(2,1)S(1)} fusion(bf16[5120,896]{1,0:T(8,128)(2,1)} %all-gather.3.cloned.1.call-done, bf16[16,5120]{1,0:T(8,128)(2,1)S(1)} %copy-done.2, f32[5120]{0:T(1024)S(1)} %convert_element_type.82, f32[16]{0:T(128)S(1)} %add_rsqrt_fusion.1, f32[896]{0:T(1024)S(1)} %convert_element_type.84), kind=kOutput, calls=%fused_computation.29 | convolution fusion | flops 147156992 | bytes 9391680 | tf_op jit(solution)/shard_map/dot_general | solution.py:115
  279.5 0.1 reshape.187
  279.6 0.1 fusion.33
  279.7 0.0 copy-done
  279.7 0.5 select_reduce_fusion
  280.2 0.2 fusion.28
  280.4 1.5 fusion.18
  281.9 0.6 copy.73
  282.6 15.4 %all-to-all-done.1 = bf16[2,64,8,896]{3,0,1,2:T(2,128)(2,1)S(1)} async-done(((bf16[2,64,8,896]{3,0,1,2:T(2,128)(2,1)}), bf16[2,64,8,896]{3,0,1,2:T(2,128)(2,1)S(1)}, u32[]{:S(2)}, u32[]{:S(2)}) %all-to-all-start.1) | async-done | bytes 1835040 | tf_op jit(solution)/shard_map/all_to_all | solution.py:140
  298.0 1.0 copy.72
  299.0 0.1 fusion.46
  299.1 0.1 slice.29
  299.2 1.2 fusion.13
  300.4 1.0 fusion.47
  301.4 0.8 fusion.12
  302.2 0.9 copy.46
  303.2 2.3 reshape.197
  (12 shorter events, 0.1 us)
Async XLA Ops:
  7.2 272.5 %copy-start = (bf16[16,1,256,128]{3,2,1,0:T(8,128)(2,1)S(1)}, bf16[16,1,256,128]{3,2,1,0:T(8,128)(2,1)}, u32[]{:S(2)}) copy-start(bf16[16,1,256,128]{3,2,1,0:T(8,128)(2,1)} %param.14) | copy-start | bytes 3145732
  7.2 17.4 %copy-start.4 = (bf16[896]{0:T(1024)(128)(2,1)S(1)}, bf16[896]{0:T(1024)(128)(2,1)}, u32[]{:S(2)}) copy-start(bf16[896]{0:T(1024)(128)(2,1)} %param.11) | copy-start | bytes 5380
  7.2 17.4 %copy-start.3 = (bf16[5120]{0:T(1024)(128)(2,1)S(1)}, bf16[5120]{0:T(1024)(128)(2,1)}, u32[]{:S(2)}) copy-start(bf16[5120]{0:T(1024)(128)(2,1)} %param.12) | copy-start | bytes 30724
  7.2 17.4 %copy-start.7 = (s32[10,1]{0,1:T(1,128)S(1)}, s32[10,1]{0,1:T(1,128)}, u32[]{:S(2)}) copy-start(s32[10,1]{0,1:T(1,128)} %param.19) | copy-start | bytes 124
  7.2 17.6 %copy-start.6 = (s32[1,10]{1,0:T(1,128)S(1)}, s32[1,10]{1,0:T(1,128)}, u32[]{:S(2)}) copy-start(s32[1,10]{1,0:T(1,128)} %param.18) | copy-start | bytes 124
  7.2 17.7 %copy-start.2 = (bf16[16,5120]{1,0:T(8,128)(2,1)S(1)}, bf16[16,5120]{1,0:T(8,128)(2,1)}, u32[]{:S(2)}) copy-start(bf16[16,5120]{1,0:T(8,128)(2,1)} %param.13) | copy-start | bytes 491524
  7.2 18.0 %copy-start.5 = (s32[1,16]{1,0:T(1,128)S(1)}, s32[1,16]{1,0:T(1,128)}, u32[]{:S(2)}) copy-start(s32[1,16]{1,0:T(1,128)} %param.16) | copy-start | bytes 196
  7.2 114.5 %all-gather.5.cloned.1.call-start = ((), (), s32[]{:S(2)}) async-start(), calls=%async_computation.3 | async-start | bytes 7372800 | tf_op jit(solution)/shard_map/all_gather | solution.py:110
  8.0 244.8 %all-gather.3.cloned.1.call-start = ((), (), s32[]{:S(2)}) async-start(), calls=%async_computation.2 | async-start | bytes 9318400 | tf_op jit(solution)/shard_map/all_gather | solution.py:114
  121.7 4.7 %copy-start.1 = (bf16[10,64,5120]{2,1,0:T(8,128)(2,1)S(1)}, bf16[10,64,5120]{2,1,0:T(8,128)(2,1)}, u32[]{:S(2)}) copy-start(bf16[10,64,5120]{2,1,0:T(8,128)(2,1)} %all-gather.5.cloned.1.call-done) | copy-start | bytes 19660804
  268.1 29.8 %all-to-all-start.1 = ((bf16[2,64,8,896]{3,0,1,2:T(2,128)(2,1)}), bf16[2,64,8,896]{3,0,1,2:T(2,128)(2,1)S(1)}, u32[]{:S(2)}, u32[]{:S(2)}) async-start(bf16[2,64,8,896]{3,0,1,2:T(2,128)(2,1)} %copy.40), calls=%async_computation.1 | async-start | bytes 3670016 | tf_op jit(solution)/shard_map/all_to_all | solution.py:140
Sparse Core Ops, SparseCore 0:
  11.3 110.3 all-gather.4
  124.4 128.2 all-gather.2
where the time goes:
time: 313 us; the launch traced here: 312 us
  waiting for transfers between devices  234 us (75%)
  matrix products  21.8 us (7%)
  blocking collectives  14.8 us (5%)
  between operations  14.3 us (5%)
  other arithmetic  11.5 us (4%)
  local copies, waits for them, and re-layouts  9.97 us (3%)
  starting transfers between devices  6.51 us (2%)
    all_gather x1, waiting for transfers between devices, body(): weight_all = lax.all_gather(blocks, 'replica', axis=0, tiled=True)  121 us
    all_gather x1, waiting for transfers between devices, body(): resp_full = lax.all_gather(response_hidden, 'tensor', axis=2, tiled=True)  96.4 us
    all_to_all x1, waiting for transfers between devices, body(): lax.all_to_all(sendbuf, 'tensor', split_axis=2, concat_axis=2, tiled=True)  15.4 us
    all_to_all x1, blocking collectives, body(): lax.all_to_all(qkv_weight.reshape(rows_local, tensor_count, col_width), '...  14.8 us
    dot_general x1, matrix products, body(): jnp.dot(resp_norm, weight_all, preferred_element_type=jnp.float32)  11.8 us
    all_to_all x1, starting transfers between devices, body(): lax.all_to_all(sendbuf, 'tensor', split_axis=2, concat_axis=2, tiled=True)  6.43 us
  transfers between devices with their start and end apart: 3, of which 3 were waited for; matrix products, arithmetic and copies ran while one was open for 6% of the time, Pallas kernels for 0%

commit v1 on v0

--- a/solution.py
+++ b/solution.py
@@ -107,7 +107,10 @@
     )
     blocks = blocks.reshape(rows_local * tensor_count, col_width)
     step_norm = normalize(decode_hidden, norm_gain)
-    resp_full = lax.all_gather(response_hidden, "tensor", axis=2, tiled=True)
+    peers = lax.axis_size("tensor")
+    pieces = jnp.stack([response_hidden for _ in range(peers)])
+    pieces = lax.all_to_all(pieces, "tensor", split_axis=0, concat_axis=0)
+    resp_full = jnp.concatenate(pieces, axis=2)
     resp_norm = normalize(resp_full, norm_gain).reshape(
         DONE_PER_GROUP * RESPONSE_LIMIT, MODEL_WIDTH
     )

time: 313 us -> 254 us (0.81)
  the two profiles are of different devices: /device:TPU:1 before, /device:TPU:480 now
where the time goes in v1:
time: 254 us
  waiting for transfers between devices  133 us (52%)
  local copies, waits for them, and re-layouts  43.6 us (17%)
  matrix products  22.8 us (9%)
  other arithmetic  15.5 us (6%)
  blocking collectives  15.3 us (6%)
  between operations  14.3 us (6%)
  starting transfers between devices  9.3 us (4%)
    all_to_all x1, waiting for transfers between devices, body(): pieces = lax.all_to_all(pieces, 'tensor', split_axis=0, concat_axis=0)  120 us
    convert_element_type x1, local copies, waits for them, and re-layouts, normalize(): widened = rows_in.astype(jnp.float32)  17.6 us
    all_to_all x1, blocking collectives, body(): lax.all_to_all(qkv_weight.reshape(rows_local, tensor_count, col_width), '...  15.3 us
    unnamed x19, local copies, waits for them, and re-layouts  14.3 us
    all_to_all x1, waiting for transfers between devices, body(): lax.all_to_all(sendbuf, 'tensor', split_axis=2, concat_axis=2, tiled=True)  13.2 us
    dot_general x1, matrix products, body(): jnp.dot(resp_norm, weight_all, preferred_element_type=jnp.float32)  12.8 us
    convert_element_type x1, other arithmetic, normalize(): widened = rows_in.astype(jnp.float32)  9.4 us
  transfers between devices with their start and end apart: 3, of which 2 were waited for; matrix products, arithmetic and copies ran while one was open for 22% of the time, Pallas kernels for 0%

profile of v1, /device:TPU:480, one launch (start us, length us, event | category | flops | bytes accessed | tf_op | source)
XLA Modules:
  0.0 253.8 jit_solution(7076216400532743673)
XLA Ops:
  7.2 0.0 copy-start
  7.2 0.0 copy-start.2
  7.2 0.0 all-gather.2.cloned.1.call-start
  7.2 1.1 copy.61
  8.4 15.3 %all_to_all.25 = bf16[10,8,896]{2,0,1:T(8,128)(2,1)S(1)} all-to-all(bf16[10,8,896]{2,0,1:T(8,128)(2,1)S(1)} %copy.40), channel_id=1, replica_groups=mesh['replica'=64,'tensor'=8] {'tensor'}, dimensions={1} | all-to-all | bytes 286720 | tf_op jit(solution)/shard_map/all_to_all | solution.py:101
  23.7 0.7 reshape.199
  24.4 0.0 all-gather.2.cloned.1.call-update
  24.4 0.0 copy-done.2
  24.5 3.7 %stack.2 = bf16[8,10,64,640]{3,2,1,0:T(8,128)(2,1)} broadcast(bf16[10,64,640]{2,1,0:T(8,128)(2,1)S(1)} %copy-done.2), dimensions={1,2,3} | broadcast | bytes 7372800 | tf_op jit(solution)/shard_map/stack | solution.py:111
  28.2 0.0 copy-start.4
  28.2 0.0 copy-start.3
  28.2 0.0 copy-start.7
  28.2 0.0 copy-start.6
  28.2 0.0 copy-start.1
  28.2 0.0 copy-start.5
  28.2 5.0 %all-to-all-start.1 = ((bf16[8,10,64,640]{3,2,1,0:T(8,128)(2,1)}), bf16[8,10,64,640]{3,2,1,0:T(8,128)(2,1)}, u32[]{:S(2)}, u32[]{:S(2)}) async-start(bf16[8,10,64,640]{3,2,1,0:T(8,128)(2,1)} %stack.2), calls=%async_computation.1 | async-start | bytes 13107200 | tf_op jit(solution)/shard_map/all_to_all | solution.py:112
  33.2 0.0 copy-done.4
  33.2 0.0 copy-done.3
  33.3 0.0 copy-done.7
  33.3 0.2 convert_reduce_fusion
  33.5 0.0 copy-done.6
  33.5 0.1 fusion.43
  33.6 0.0 copy-done.1
  33.6 0.2 fusion.23
  33.8 0.1 iota_compare_fusion.3
  33.8 0.0 copy-done.5
  33.8 0.1 iota_compare_fusion.1
  33.9 119.8 %all-to-all-done.1 = bf16[8,10,64,640]{3,2,1,0:T(8,128)(2,1)} async-done(((bf16[8,10,64,640]{3,2,1,0:T(8,128)(2,1)}), bf16[8,10,64,640]{3,2,1,0:T(8,128)(2,1)}, u32[]{:S(2)}, u32[]{:S(2)}) %all-to-all-start.1) | async-done | bytes 6553632 | tf_op jit(solution)/shard_map/all_to_all | solution.py:112
  153.7 4.2 %fusion.1 = f32[10,64]{1,0:T(8,128)S(1)} fusion(bf16[8,10,64,640]{3,2,1,0:T(8,128)(2,1)} %all-to-all-done.1), kind=kLoop, calls=%fused_computation.3 | loop fusion | flops 9829760 | bytes 6556160 | tf_op jit(solution)/shard_map/reduce_sum | solution.py:17
  158.0 0.1 rsqrt.21
  158.0 9.4 %convert_bitcast_fusion = f32[10,64,8,640]{3,1,0,2:T(8,128)} fusion(bf16[8,10,64,640]{3,2,1,0:T(8,128)(2,1)} %all-to-all-done.1), kind=kLoop, calls=%fused_computation.2 | loop fusion | flops 3276800 | bytes 19660800 | tf_op jit(solution)/shard_map/convert_element_type | solution.py:16
  167.4 17.6 %copy.41 = f32[10,64,8,640]{3,2,1,0:T(8,128)} copy(f32[10,64,8,640]{3,1,0,2:T(8,128)} %convert_bitcast_fusion) | data formatting | bytes 26214400 | tf_op jit(solution)/shard_map/convert_element_type | solution.py:16
  185.0 12.5 %copy.63 = f32[80,8,8,640]{3,1,2,0:T(8,128)} copy(f32[80,8,8,640]{3,2,1,0:T(8,128)} %bitcast.82) | data formatting | bytes 26214400
  197.5 0.0 all-gather.2.cloned.1.call-done
  197.5 12.8 %add_convert_fusion = bf16[640,896]{1,0:T(8,128)(2,1)S(1)} fusion(bf16[5120,896]{1,0:T(8,128)(2,1)} %all-gather.2.cloned.1.call-done, f32[640,5120]{1,0:T(8,128)} %bitcast.83, f32[5120]{0:T(1024)S(1)} %convert_element_type.94, f32[640]{0:T(1024)S(1)} %rsqrt.21, f32[896]{0:T(1024)S(1)} %convert_element_type.96), kind=kOutput, calls=%fused_computation.16 | convolution fusion | flops 5883002880 | bytes 23455744 | tf_op jit(solution)/shard_map/dot_general | solution.py:119
  210.3 0.9 convert_bitcast_fusion.1
  211.3 2.7 %copy.43 = bf16[2,64,8,896]{3,0,1,2:T(2,128)(2,1)} copy(bf16[2,64,8,896]{3,2,0,1:T(8,128)(2,1)S(1)} %convert_bitcast_fusion.1) | data formatting | bytes 3670016 | tf_op jit(solution)/shard_map/convert_element_type | solution.py:142
  213.9 4.3 %all-to-all-start.2 = ((bf16[2,64,8,896]{3,0,1,2:T(2,128)(2,1)}), bf16[2,64,8,896]{3,0,1,2:T(2,128)(2,1)S(1)}, u32[]{:S(2)}, u32[]{:S(2)}) async-start(bf16[2,64,8,896]{3,0,1,2:T(2,128)(2,1)} %copy.43), calls=%async_computation.2 | async-start | bytes 3670016 | tf_op jit(solution)/shard_map/all_to_all | solution.py:143
  218.2 4.9 %fusion.20 = bf16[16,896]{1,0:T(8,128)(2,1)S(1)} fusion(bf16[5120,896]{1,0:T(8,128)(2,1)} %all-gather.2.cloned.1.call-done, bf16[16,5120]{1,0:T(8,128)(2,1)S(1)} %copy-done.1, f32[5120]{0:T(1024)S(1)} %convert_element_type.94, f32[16]{0:T(128)S(1)} %add_rsqrt_fusion.1, f32[896]{0:T(1024)S(1)} %convert_element_type.96), kind=kOutput, calls=%fused_computation.31 | convolution fusion | flops 147156992 | bytes 9391680 | tf_op jit(solution)/shard_map/dot_general | solution.py:118
  223.2 0.1 reshape.200
  223.2 0.1 fusion.34
  223.4 0.0 copy-done
  223.4 0.5 select_reduce_fusion
  223.9 0.2 fusion.29
  224.1 1.5 fusion.19
  225.6 0.6 copy.77
  226.2 13.2 %all-to-all-done.2 = bf16[2,64,8,896]{3,0,1,2:T(2,128)(2,1)S(1)} async-done(((bf16[2,64,8,896]{3,0,1,2:T(2,128)(2,1)}), bf16[2,64,8,896]{3,0,1,2:T(2,128)(2,1)S(1)}, u32[]{:S(2)}, u32[]{:S(2)}) %all-to-all-start.2) | async-done | bytes 1835040 | tf_op jit(solution)/shard_map/all_to_all | solution.py:143
  239.5 1.0 copy.76
  240.5 0.1 fusion.47
  240.6 0.1 slice.29
  240.7 1.2 fusion.14
  241.9 1.0 fusion.48
  242.9 0.8 fusion.13
  243.7 0.9 copy.49
  244.7 2.3 reshape.209
  (12 shorter events, 0.1 us)
Async XLA Ops:
  7.2 216.2 %copy-start = (bf16[16,1,256,128]{3,2,1,0:T(8,128)(2,1)S(1)}, bf16[16,1,256,128]{3,2,1,0:T(8,128)(2,1)}, u32[]{:S(2)}) copy-start(bf16[16,1,256,128]{3,2,1,0:T(8,128)(2,1)} %param.14) | copy-start | bytes 3145732
  7.2 17.3 %copy-start.2 = (bf16[10,64,640]{2,1,0:T(8,128)(2,1)S(1)}, bf16[10,64,640]{2,1,0:T(8,128)(2,1)}, u32[]{:S(2)}) copy-start(bf16[10,64,640]{2,1,0:T(8,128)(2,1)} %param.17) | copy-start | bytes 2457604
  7.2 190.3 %all-gather.2.cloned.1.call-start = ((), (), s32[]{:S(2)}) async-start(), calls=%async_computation.3 | async-start | bytes 9318400 | tf_op jit(solution)/shard_map/all_gather | solution.py:117
  28.2 5.0 %copy-start.4 = (bf16[896]{0:T(1024)(128)(2,1)S(1)}, bf16[896]{0:T(1024)(128)(2,1)}, u32[]{:S(2)}) copy-start(bf16[896]{0:T(1024)(128)(2,1)} %param.11) | copy-start | bytes 5380
  28.2 5.0 %copy-start.3 = (bf16[5120]{0:T(1024)(128)(2,1)S(1)}, bf16[5120]{0:T(1024)(128)(2,1)}, u32[]{:S(2)}) copy-start(bf16[5120]{0:T(1024)(128)(2,1)} %param.12) | copy-start | bytes 30724
  28.2 5.1 %copy-start.7 = (s32[10,1]{0,1:T(1,128)S(1)}, s32[10,1]{0,1:T(1,128)}, u32[]{:S(2)}) copy-start(s32[10,1]{0,1:T(1,128)} %param.19) | copy-start | bytes 124
  28.2 5.3 %copy-start.6 = (s32[1,10]{1,0:T(1,128)S(1)}, s32[1,10]{1,0:T(1,128)}, u32[]{:S(2)}) copy-start(s32[1,10]{1,0:T(1,128)} %param.18) | copy-start | bytes 124
  28.2 5.4 %copy-start.1 = (bf16[16,5120]{1,0:T(8,128)(2,1)S(1)}, bf16[16,5120]{1,0:T(8,128)(2,1)}, u32[]{:S(2)}) copy-start(bf16[16,5120]{1,0:T(8,128)(2,1)} %param.13) | copy-start | bytes 491524
  28.2 5.6 %copy-start.5 = (s32[1,16]{1,0:T(1,128)S(1)}, s32[1,16]{1,0:T(1,128)}, u32[]{:S(2)}) copy-start(s32[1,16]{1,0:T(1,128)} %param.16) | copy-start | bytes 196
  28.2 125.5 %all-to-all-start.1 = ((bf16[8,10,64,640]{3,2,1,0:T(8,128)(2,1)}), bf16[8,10,64,640]{3,2,1,0:T(8,128)(2,1)}, u32[]{:S(2)}, u32[]{:S(2)}) async-start(bf16[8,10,64,640]{3,2,1,0:T(8,128)(2,1)} %stack.2), calls=%async_computation.1 | async-start | bytes 13107200 | tf_op jit(solution)/shard_map/all_to_all | solution.py:112
  213.9 25.5 %all-to-all-start.2 = ((bf16[2,64,8,896]{3,0,1,2:T(2,128)(2,1)}), bf16[2,64,8,896]{3,0,1,2:T(2,128)(2,1)S(1)}, u32[]{:S(2)}, u32[]{:S(2)}) async-start(bf16[2,64,8,896]{3,0,1,2:T(2,128)(2,1)} %copy.43), calls=%async_computation.2 | async-start | bytes 3670016 | tf_op jit(solution)/shard_map/all_to_all | solution.py:143
Sparse Core Ops, SparseCore 0:
  24.6 121.5 all-gather.1
